TPU v7x, 256 devices: a whole 4x4x8 slice. The times are simulated.
256 devices in a mesh: region: 32 (over z, y), rays: 8 (over x, core).
Axes of the slice: x: 4, y: 4, z: 8, core: 2. Of those that a mesh axis runs over, the one named last changes fastest.
Arguments:
- grid_coords: int32 [3, 32, 4, 32768], P(None, 'region', None, 'rays'), may hold values from 0 to 4095
- segment_bounds: int32 [2, 32, 32768], P(None, 'region', 'rays'), may hold values from 0 to 4, as said below
- depth_rank: int32 [32768, 32], P('rays'), may hold values from 0 to 31, each once within a row
- step_length: float32 [32, 4, 32768], P('region', None, 'rays'), may hold values from 0.01 to 0.08
- sample_depth: float32 [32, 4, 32768], P('region', None, 'rays'), may hold values from 0.5 to 4
- target_pixels: float32 [4, 32768], P(None, 'rays'), may hold values from 0 to 1.5
- weight_in: bfloat16 [32, 60, 256], P('region'), may hold values from -0.75 to 0.75
- weight_mid: bfloat16 [32, 256, 256], P('region'), may hold values from -0.375 to 0.375
- weight_out: bfloat16 [32, 4, 256], P('region'), may hold values from -0.375 to 0.375
- bias_hidden: float32 [32, 2, 256], P('region'), may hold values from -3 to 3
Outputs:
- grad_in: float32 [32, 60, 256], P('region', None, 'rays')
- grad_mid: float32 [32, 256, 256], P('region', None, 'rays')
- grad_out: float32 [32, 4, 256], P('region', None, 'rays')
- grad_bias: float32 [32, 2, 256], P('region', None, 'rays')
Inputs may be any that keep to these rules, and one draw needn't show every extreme that they name: For every region and ray segment_bounds[0] <= segment_bounds[1]; the ray's live samples in the region are the slots from segment_bounds[0] to segment_bounds[1] - 1; in every region some ray has all 4 slots live.
All inputs are finite; a program needn't handle non-finite values.
Results may differ from a plain program's by a relative error of at most 0.00055.
Values sent between devices are 32-bit elements; how exact they have to be, the bound alone decides.
No kernel may reach another device: no remote copies, remote signals or barrier semaphores. Data moves between devices by JAX's collectives and lax.ppermute only.
A program may use at most 128 MiB of HBM per device.

v0:
```python
import math

import jax
import jax.numpy as jnp
from jax import lax
from jax.sharding import PartitionSpec as P

GRID = 4096


depth_weight = 0.1


def encode(coords, freq_count):
    position = (coords.astype(jnp.float32) + 0.5) / GRID
    position = position.reshape(3, -1)
    scales = 2.0 ** lax.broadcasted_iota(jnp.float32, (freq_count, 1, 1), 0) * math.pi
    angle = scales * position[None]
    both = jnp.concatenate([jnp.sin(angle), jnp.cos(angle)], axis=0)
    return both.reshape(6 * freq_count, -1).astype(jnp.bfloat16)


def silu_slope(value):
    sig = jax.nn.sigmoid(value)
    return sig * (1.0 + value * (1.0 - sig))


def forward(
    weight_in, weight_mid, weight_out, bias_hidden, coords, bounds, step_length, sample_depth
):
    slots, rays = step_length.shape
    encoded = encode(coords, weight_in.shape[0] // 6)
    contract = (((0,), (0,)), ((), ()))
    pre_one = (
        lax.dot_general(weight_in, encoded, contract, preferred_element_type=jnp.float32)
        + bias_hidden[0][:, None]
    )
    hidden_one = jax.nn.silu(pre_one).astype(jnp.bfloat16)
    pre_two = (
        lax.dot_general(weight_mid, hidden_one, contract, preferred_element_type=jnp.float32)
        + bias_hidden[1][:, None]
    )
    hidden_two = jax.nn.silu(pre_two).astype(jnp.bfloat16)
    raw_out = jnp.dot(weight_out, hidden_two, preferred_element_type=jnp.float32).reshape(
        4, slots, rays
    )
    density = jax.nn.softplus(raw_out[0])
    colour = jax.nn.sigmoid(raw_out[1:])
    slot_index = lax.broadcasted_iota(jnp.int32, (slots, rays), 0)
    live_mask = ((slot_index >= bounds[0][None]) & (slot_index < bounds[1][None])).astype(
        jnp.float32
    )
    optical = density * step_length * live_mask
    optical_before = jnp.cumsum(optical, axis=0) - optical
    blend = jnp.exp(-optical_before) * -jnp.expm1(-optical)
    segment_colour = jnp.sum(blend[None] * colour, axis=1)
    segment_depth = jnp.sum(blend * sample_depth, axis=0)
    log_passing = -jnp.sum(optical, axis=0)
    segment = jnp.concatenate([segment_colour, segment_depth[None], log_passing[None]], axis=0)
    cache = (
        encoded,
        pre_one,
        hidden_one,
        pre_two,
        hidden_two,
        raw_out,
        colour,
        live_mask,
        optical,
        optical_before,
        blend,
    )
    return (segment, cache)


def backward(weight_mid, weight_out, step_length, sample_depth, cache, grad_segment):
    (
        encoded,
        pre_one,
        hidden_one,
        pre_two,
        hidden_two,
        raw_out,
        colour,
        live_mask,
        optical,
        optical_before,
        blend,
    ) = cache
    grad_colour = grad_segment[:3]
    usage_grad = (
        jnp.sum(grad_colour[:, None] * colour, axis=0) + grad_segment[3][None] * sample_depth
    )
    weighted = usage_grad * blend
    later_sum = jnp.sum(weighted, axis=0)[None] - jnp.cumsum(weighted, axis=0)
    grad_optical = (
        usage_grad * jnp.exp(-(optical_before + optical)) - later_sum - grad_segment[4][None]
    )
    grad_density = grad_optical * step_length * live_mask * jax.nn.sigmoid(raw_out[0])
    grad_hue = grad_colour[:, None] * blend[None] * colour * (1.0 - colour)
    grad_raw = (
        jnp.concatenate([grad_density[None], grad_hue], axis=0).reshape(4, -1).astype(jnp.bfloat16)
    )
    contract = (((0,), (0,)), ((), ()))
    over_samples = (((1,), (1,)), ((), ()))
    grad_out = lax.dot_general(
        grad_raw, hidden_two, over_samples, preferred_element_type=jnp.float32
    )
    grad_pre_two = lax.dot_general(
        weight_out, grad_raw, contract, preferred_element_type=jnp.float32
    ) * silu_slope(pre_two)
    rounded_two = grad_pre_two.astype(jnp.bfloat16)
    grad_mid = lax.dot_general(
        hidden_one, rounded_two, over_samples, preferred_element_type=jnp.float32
    )
    grad_pre_one = jnp.dot(
        weight_mid, rounded_two, preferred_element_type=jnp.float32
    ) * silu_slope(pre_one)
    rounded_one = grad_pre_one.astype(jnp.bfloat16)
    grad_in = lax.dot_general(
        encoded, rounded_one, over_samples, preferred_element_type=jnp.float32
    )
    grad_bias = jnp.stack([jnp.sum(grad_pre_one, axis=1), jnp.sum(grad_pre_two, axis=1)])
    return (grad_in, grad_mid, grad_out, grad_bias)


def loss_slope(composite_vals, target, loss_scale):
    gains = jnp.array([1.0, 1.0, 1.0, depth_weight], jnp.float32)
    return 2.0 * loss_scale * gains[:, None] * (composite_vals - target)


def join_segments(segments, depth_ranks, target, loss_scale):
    log_passing = segments[4]
    earlier = depth_ranks[None] < depth_ranks[:, None]
    light_before = jnp.exp(jnp.sum(jnp.where(earlier, log_passing[None], 0.0), axis=1))
    composite_vals = jnp.sum(light_before[None] * segments[:4], axis=1)
    grad_composite = loss_slope(composite_vals, target, loss_scale)
    light_terms = light_before * jnp.sum(grad_composite[:, None] * segments[:4], axis=0)
    later_terms = jnp.sum(jnp.where(earlier, light_terms[:, None], 0.0), axis=0)
    return jnp.concatenate(
        [light_before[None] * grad_composite[:, None], later_terms[None]], axis=0
    )


def on_device(
    grid_coords,
    segment_bounds,
    depth_rank,
    step_length,
    sample_depth,
    target_pixels,
    weight_in,
    weight_mid,
    weight_out,
    bias_hidden,
):
    segment, cache = forward(
        weight_in[0],
        weight_mid[0],
        weight_out[0],
        bias_hidden[0],
        grid_coords[:, 0],
        segment_bounds[:, 0],
        step_length[0],
        sample_depth[0],
    )
    ray_count = depth_rank.shape[0]
    loss_scale = 1.0 / math.sqrt(ray_count * lax.axis_size("rays"))
    position = lax.axis_index("region")
    gathered = lax.all_gather(segment[:, None], "region", axis=1, tiled=True)
    all_grads = join_segments(gathered, depth_rank.T, target_pixels, loss_scale)
    segment_grad = lax.dynamic_index_in_dim(all_grads, position, 1, keepdims=False)
    grad_in, grad_mid, grad_out, grad_bias = backward(
        weight_mid[0], weight_out[0], step_length[0], sample_depth[0], cache, segment_grad
    )
    grad_in, grad_mid, grad_out, grad_bias = (
        lax.psum_scatter(grad_in[None], "rays", scatter_dimension=2, tiled=True),
        lax.psum_scatter(grad_mid[None], "rays", scatter_dimension=2, tiled=True),
        lax.psum_scatter(grad_out[None], "rays", scatter_dimension=2, tiled=True),
        lax.psum_scatter(grad_bias[None], "rays", scatter_dimension=2, tiled=True),
    )
    return (grad_in, grad_mid, grad_out, grad_bias)


def solution(mesh):
    placed = (
        P(None, "region", None, "rays"),
        P(None, "region", "rays"),
        P("rays", None),
        P("region", None, "rays"),
        P("region", None, "rays"),
        P(None, "rays"),
        P("region", None, None),
        P("region", None, None),
        P("region", None, None),
        P("region", None, None),
    )
    return jax.shard_map(
        on_device,
        mesh=mesh,
        in_specs=placed,
        out_specs=(
            P("region", None, "rays"),
            P("region", None, "rays"),
            P("region", None, "rays"),
            P("region", None, "rays"),
        ),
        check_vma=False,
    )
```

profile of v0, /device:TPU:8, one launch (start us, length us, event | category | flops | bytes accessed | tf_op | source)
XLA Modules:
  0.0 368.1 jit_solution(18266262084740102157)
XLA Ops:
  7.2 0.0 copy-start
  7.2 0.0 all-gather.3.cloned.1.call-start
  7.2 1.0 multiply_bitcast_fusion
  8.2 0.1 copy.32
  8.4 19.1 %multiply_sine_fusion = (bf16[10,3,16384]{2,1,0:T(4,128)(2,1)S(1)}, bf16[10,3,16384]{2,1,0:T(4,128)(2,1)S(1)}) fusion(f32[3,16384]{1,0:T(4,128)S(1)} %bitcast.120, f32[10]{0:T(128)S(1)} %power_multiply_fusion), kind=kLoop, calls=%fused_computation.26 | loop fusion | flops 1474560 | bytes 2162728 | tf_op jit(solution)/shard_map/sin | solution.py:19
  27.5 3.2 maximum_convert_fusion
  30.7 3.4 convert_element_type.37
  34.1 0.8 fusion.41
  34.8 8.9 %fusion.1 = f32[256,16384]{0,1:T(8,128)} fusion(bf16[60,16384]{1,0:T(8,128)(2,1)S(1)} %convert_element_type.37, f32[256]{0:T(256)S(1)} %bitcast.143, bf16[1,60,256]{2,1,0:T(8,128)(2,1)} %param.17), kind=kOutput, calls=%fused_computation.4 | convolution fusion | flops 507510784 | bytes 18775040 | tf_op jit(solution)/shard_map/dot_general | solution.py:35
  43.8 15.4 %multiply_convert_fusion = (bf16[256,16384]{0,1:T(8,128)(2,1)S(1)}, f32[256,16384]{0,1:T(8,128)}) fusion(f32[256]{0:T(256)S(1)} %bitcast.145, bf16[1,256,256]{2,1,0:T(8,128)(2,1)S(1)} %copy-done, f32[256,16384]{0,1:T(8,128)} %fusion.1), kind=kOutput, calls=%fused_computation.13 | convolution fusion | flops 2193620992 | bytes 42075136 | tf_op jit(solution)/shard_map/dot_general | solution.py:40
  59.2 3.2 copy-done.2
  62.4 2.3 convolution_bitcast_fusion.2
  64.6 0.2 fusion.38
  64.8 0.1 fusion.16
  65.1 0.2 div.41
  65.3 0.1 fusion.21
  65.4 0.1 reduce_window_sum.19
  65.5 0.2 negate_multiply_fusion.1
  65.7 0.1 fusion.24
  65.8 0.1 multiply_reduce_fusion.3
  66.0 0.7 pad_maximum_fusion
  66.7 0.0 all-gather.3.cloned.1.call-update
  66.7 0.3 reduce-scatter.12.cloned.1.call-start
  67.0 83.3 %all-gather.3.cloned.1.call-done = f32[5,131072]{1,0:T(8,128)} async-done(((f32[5,4096]{1,0:T(8,128)}), f32[5,131072]{1,0:T(8,128)}) %all-gather.3.cloned.1.call-update) | async-done | bytes 2621456 | tf_op jit(solution)/shard_map/all_gather | solution.py:170
  150.3 3.7 %slice_reduce_fusion = f32[131072]{0:T(1024)S(1)} fusion(f32[5,131072]{1,0:T(8,128)} %all-gather.3.cloned.1.call-done), kind=kLoop, calls=%fused_computation.32 | loop fusion | bytes 1048576 | tf_op jit(solution)/shard_map/slice | solution.py:133
  154.0 0.1 broadcast_in_dim.62
  154.1 2.5 fusion.4
  156.7 0.1 exp.69
  156.7 2.5 slice.60
  159.3 0.5 multiply_reduce_fusion.1
  159.8 0.1 subtract_multiply_fusion
  159.9 2.3 multiply_reduce_fusion
  162.2 0.1 exponential_multiply_fusion
  162.3 2.0 fusion.5
  164.3 0.5 copy.23
  165.0 0.1 copy.33
  165.2 0.4 multiply_reduce_fusion.2
  165.6 0.1 fusion.27
  165.7 0.1 reduce_window_sum.21
  165.9 0.2 fusion.32
  166.0 0.1 copy.34
  166.1 10.2 %fusion.42 = (f32[256]{0:T(256)S(1)}, bf16[256,16384]{0,1:T(8,128)(2,1)S(1)}) fusion(f32[256,16384]{0,1:T(8,128)} %get-tuple-element.37, bf16[1,4,256]{2,1,0:T(4,128)(2,1)S(1)} %copy-done.10, bf16[3,16384]{1,0:T(4,128)(2,1)S(1)} %get-tuple-element.23, bf16[1,16384]{1,0:T(2,128)(2,1)S(1)} %bitcast.125), kind=kOutput, calls=%fused_computation.89 | convolution fusion | flops 75759360 | bytes 25299968 | tf_op jit(solution)/shard_map/dot_general | solution.py:109
  176.3 16.2 %fusion.43 = (f32[256]{0:T(256)S(1)}, bf16[256,16384]{0,1:T(8,128)(2,1)}) fusion(f32[256,16384]{0,1:T(8,128)} %fusion.1, bf16[1,256,256]{2,1,0:T(8,128)(2,1)S(1)} %copy-done, bf16[256,16384]{0,1:T(8,128)(2,1)S(1)} %get-tuple-element.39), kind=kOutput, calls=%fused_computation.90 | convolution fusion | flops 2189426432 | bytes 33686528 | tf_op jit(solution)/shard_map/dot_general | solution.py:116
  192.5 0.8 copy.30
  193.3 0.0 reduce-scatter.12.cloned.1.call-update
  193.3 0.0 reduce-scatter.10.cloned.1.call-start
  193.3 7.4 %convolution_bitcast_fusion.3 = f32[256,4]{1,0:T(8,128)} fusion(bf16[256,16384]{0,1:T(8,128)(2,1)} %copy-done.2, bf16[3,16384]{1,0:T(4,128)(2,1)S(1)} %get-tuple-element.23, bf16[1,16384]{1,0:T(2,128)(2,1)S(1)} %bitcast.126), kind=kOutput, calls=%fused_computation.30 | convolution fusion | flops 33816576 | bytes 8523776 | tf_op jit(solution)/shard_map/dot_general | solution.py:106
  200.7 0.0 reduce-scatter.10.cloned.1.call-update
  200.8 0.0 all-reduce.3.cloned.1.call-start
  200.8 10.7 %fusion.11 = f32[1,256,256]{2,1,0:T(8,128)S(1)} fusion(bf16[256,16384]{0,1:T(8,128)(2,1)} %copy-done.13, f32[256,16384]{0,1:T(8,128)} %fusion.1), kind=kOutput, calls=%fused_computation.29 | convolution fusion | flops 2168455168 | bytes 25427968 | tf_op jit(solution)/shard_map/dot_general | solution.py:113
  211.6 0.8 copy.25
  212.4 0.0 all-reduce.3.cloned.1.call-update
  212.4 0.3 reduce-scatter.8.cloned.1.call-start
  212.8 7.4 %fusion.6 = f32[60,256]{0,1:T(8,128)} fusion(bf16[60,16384]{1,0:T(8,128)(2,1)S(1)} %copy-done.4, bf16[256,16384]{0,1:T(8,128)(2,1)} %get-tuple-element.41), kind=kOutput, calls=%fused_computation.17 | convolution fusion | flops 503316480 | bytes 10416128 | tf_op jit(solution)/shard_map/dot_general | solution.py:120
  220.2 0.0 reduce-scatter.8.cloned.1.call-update
  220.3 0.6 dynamic-slice
  221.5 3.2 reduce-scatter.12.cloned.1.call-done
  224.7 1.4 copy.31
  226.0 33.3 %reduce-scatter.10.cloned.1.call-done = f32[32,4]{1,0:T(8,128)} async-done(((f32[256,4]{1,0:T(8,128)}), f32[32,4]{1,0:T(8,128)}) %reduce-scatter.10.cloned.1.call-update) | async-done | bytes 528
  259.3 1.4 copy.29
  260.7 65.1 %all-reduce.3.cloned.1.call-done = f32[1,256,256]{1,0,2:T(1,128)} async-done(((f32[1,256,256]{1,0,2:T(1,128)}), f32[1,256,256]{1,0,2:T(1,128)}) %all-reduce.3.cloned.1.call-update) | async-done | bytes 262160
  325.8 0.8 constant_dynamic-slice_fusion
  326.5 0.6 copy.27
  327.1 34.0 %reduce-scatter.8.cloned.1.call-done = f32[1,60,32]{1,0,2:T(1,128)} async-done(((f32[1,60,256]{1,0,2:T(1,128)}), f32[1,60,32]{1,0,2:T(1,128)}) %reduce-scatter.8.cloned.1.call-update) | async-done | bytes 7696 | tf_op jit(solution)/shard_map/reduce_scatter | solution.py:177
  (40 shorter events, 0.4 us)
Async XLA Ops:
  7.2 36.5 %copy-start = (bf16[1,256,256]{2,1,0:T(8,128)(2,1)S(1)}, bf16[1,256,256]{2,1,0:T(8,128)(2,1)}, u32[]{:S(2)}) copy-start(bf16[1,256,256]{2,1,0:T(8,128)(2,1)} %param.18) | copy-start | bytes 393220
  7.2 143.1 %all-gather.3.cloned.1.call-start = ((), (), s32[]{:S(2)}) async-start(), calls=%async_computation.4 | async-start | bytes 4325376 | tf_op jit(solution)/shard_map/all_gather | solution.py:170
  34.1 9.6 %copy-start.3 = (bf16[60,16384]{1,0:T(8,128)(2,1)}, bf16[60,16384]{1,0:T(8,128)(2,1)S(1)}, u32[]{:S(2)}) copy-start(bf16[60,16384]{1,0:T(8,128)(2,1)S(1)} %convert_element_type.37) | copy-start | bytes 5898244
  43.7 18.7 %copy-start.10 = (bf16[1,4,256]{2,1,0:T(4,128)(2,1)S(1)}, bf16[1,4,256]{2,1,0:T(4,128)(2,1)}, u32[]{:S(2)}) copy-start(bf16[1,4,256]{2,1,0:T(4,128)(2,1)} %param.19) | copy-start | bytes 6148
  43.7 21.3 %copy-start.9 = (s32[2,1,4096]{2,1,0:T(1,128)S(1)}, s32[2,1,4096]{2,1,0:T(1,128)}, u32[]{:S(2)}) copy-start(s32[2,1,4096]{2,1,0:T(1,128)} %param.12) | copy-start | bytes 98308
  43.7 21.6 %copy-start.7 = (f32[1,4,4096]{2,1,0:T(4,128)S(1)}, f32[1,4,4096]{2,1,0:T(4,128)}, u32[]{:S(2)}) copy-start(f32[1,4,4096]{2,1,0:T(4,128)} %param.14) | copy-start | bytes 196612
  43.7 21.9 %copy-start.6 = (f32[1,4,4096]{2,1,0:T(4,128)S(1)}, f32[1,4,4096]{2,1,0:T(4,128)}, u32[]{:S(2)}) copy-start(f32[1,4,4096]{2,1,0:T(4,128)} %param.15) | copy-start | bytes 196612
  43.7 110.4 %copy-start.5 = (s32[4096,32]{0,1:T(8,128)S(1)}, s32[4096,32]{0,1:T(8,128)}, u32[]{:S(2)}) copy-start(s32[4096,32]{0,1:T(8,128)} %param.13) | copy-start | bytes 1572868
  59.2 3.2 copy-start.2
  59.2 100.6 %copy-start.8 = (f32[4,4096]{1,0:T(4,128)S(1)}, f32[4,4096]{1,0:T(4,128)}, u32[]{:S(2)}) copy-start(f32[4,4096]{1,0:T(4,128)} %param.16) | copy-start | bytes 196612
  59.2 100.6 %copy-start.11 = (f32[4]{0:T(128)S(1)}, f32[4]{0:T(128)}, u32[]{:S(2)}) copy-start(f32[4]{0:T(128)} %constant.51) | copy-start | bytes 52
  66.7 158.0 %reduce-scatter.12.cloned.1.call-start = ((), (), s32[]{:S(2)}) async-start(), calls=%async_computation.6 | async-start | bytes 147456
  176.3 16.2 %copy-start.13 = (bf16[256,16384]{0,1:T(8,128)(2,1)}, bf16[256,16384]{0,1:T(8,128)(2,1)S(1)}, u32[]{:S(2)}) copy-start(bf16[256,16384]{0,1:T(8,128)(2,1)S(1)} %get-tuple-element.39) | copy-start | bytes 25165828
  193.3 66.0 %reduce-scatter.10.cloned.1.call-start = ((), (), s32[]{:S(2)}) async-start(), calls=%async_computation.5 | async-start | bytes 147456
  200.7 12.0 %copy-start.4 = (bf16[60,16384]{1,0:T(8,128)(2,1)S(1)}, bf16[60,16384]{1,0:T(8,128)(2,1)}, u32[]{:S(2)}) copy-start(bf16[60,16384]{1,0:T(8,128)(2,1)} %copy-done.3) | copy-start | bytes 5898244
  200.8 19.5 %copy-start.12 = (u32[256]{0:T(256)S(1)}, u32[256]{0:T(256)}, u32[]{:S(2)}) copy-start(u32[256]{0:T(256)} %constant.54) | copy-start | bytes 3076
  200.8 125.0 %all-reduce.3.cloned.1.call-start = ((), (), s32[]{:S(2)}) async-start(), calls=%async_computation.7 | async-start | bytes 524288
  200.8 160.3 %copy-start.1 = (bf16[1,256,256]{2,1,0:T(8,128)(2,1)S(1)}, bf16[1,256,256]{2,1,0:T(8,128)(2,1)}, u32[]{:S(2)}) copy-start(bf16[1,256,256]{2,1,0:T(8,128)(2,1)} %param.18) | copy-start | bytes 393220
  212.4 148.6 %reduce-scatter.8.cloned.1.call-start = ((), (), s32[]{:S(2)}) async-start(), calls=%async_computation.3 | async-start | bytes 147456 | tf_op jit(solution)/shard_map/reduce_scatter | solution.py:177
Sparse Core Ops, SparseCore 0:
  66.8 83.4 all-gather.2
  193.4 31.2 reduce-scatter.11
  227.2 32.0 reduce-scatter.9
  261.5 64.2 all-reduce.2
  328.7 32.3 reduce-scatter.7
where the time goes:
time: 375 us; the launch traced here: 368 us
  waiting for transfers between devices  219 us (58%)
  matrix products  78.4 us (21%)
  other arithmetic  33.2 us (9%)
  local copies, waits for them, and re-layouts  21.6 us (6%)
  between operations  15.3 us (4%)
    unnamed x8, waiting for transfers between devices  102 us
    all_gather x1, waiting for transfers between devices, on_device(): gathered = lax.all_gather(segment[:, None], 'region', axis=1, tiled=True)  83.3 us
    reduce_scatter x1, waiting for transfers between devices, on_device(): lax.psum_scatter(grad_in[None], 'rays', scatter_dimension=2, tiled=True)  34 us
    sin x1, other arithmetic, encode(): both = jnp.concatenate([jnp.sin(angle), jnp.cos(angle)], axis=0)  19.1 us
    dot_general x1, matrix products, backward(): jnp.dot(weight_mid, rounded_two, preferred_element_type=jnp.float32)  16.2 us
    dot_general x1, matrix products, forward(): lax.dot_general(weight_mid, hidden_one, contract, preferred_element_type=...  15.4 us
    dot_general x1, matrix products, backward(): lax.dot_general(hidden_one, rounded_two, over_samples, preferred_element_...  10.7 us
    dot_general x1, matrix products, backward(): lax.dot_general(weight_out, grad_raw, contract, preferred_element_type=jn...  10.2 us
  transfers between devices with their start and end apart: 5, of which 5 were waited for; matrix products, arithmetic and copies ran while one was open for 8% of the time, Pallas kernels for 0%

commit v1 on v0

v1 whole, which is shorter than its diff:
```python
import functools
import math

import jax
import jax.numpy as jnp
from jax import lax
from jax.experimental import pallas as pl
from jax.experimental.pallas import tpu as pltpu
from jax.sharding import PartitionSpec as P

GRID = 4096
LANES = 128
DEPTH_WEIGHT = 0.1
ENC_ROWS = 64

PI_HI = 3.140625
PI_MID = 9.67502593994140625e-4
PI_LO = 1.509957990978376432e-7

SIN_COEFS = (3.1415925798055784, -5.167706866167917, 2.5500311935189344, -0.5980441939097795, 0.07721838615261653)
COS_COEFS = (-4.934795324080539, 4.058447258699471, -1.332068065877436, 0.2200300516248938)

NT = (((1,), (1,)), ((), ()))


def dot(a, b):
    return jnp.dot(a, b, preferred_element_type=jnp.float32)


def dot_nt(a, b):
    return lax.dot_general(a, b, NT, preferred_element_type=jnp.float32)


def sigmoid(x):
    return 1.0 / (1.0 + jnp.exp(-x))


def softplus(x):
    z = jnp.exp(-jnp.abs(x))
    y = z / (2.0 + z)
    q = y * y
    series = 1.0 / 15.0
    for k in (13, 11, 9, 7, 5, 3, 1):
        series = series * q + 1.0 / k
    return jnp.maximum(x, 0.0) + 2.0 * y * series


def one_less_exp(x):
    small = 1.0 / 5040.0
    for k in (720, 120, 24, 6, 2, 1):
        small = 1.0 / k - x * small
    return jnp.where(x < 0.25, x * small, 1.0 - jnp.exp(-x))


def shift_down(rows):
    total = rows[0:1]
    out = [jnp.zeros_like(total), total]
    for s in range(1, rows.shape[0] - 1):
        total = total + rows[s : s + 1]
        out.append(total)
    return jnp.concatenate(out, axis=0)


def ray_terms(raw, step, first, last):
    slot = lax.broadcasted_iota(jnp.int32, step.shape, 0)
    live = ((slot >= first) & (slot < last)).astype(jnp.float32)
    density = softplus(raw[0])
    colour = [sigmoid(raw[c]) for c in (1, 2, 3)]
    optical = density * step * live
    before = shift_down(optical)
    blend = jnp.exp(-before) * one_less_exp(optical)
    return live, colour, optical, before, blend


def row_sum(x):
    return jnp.sum(x, axis=0, keepdims=True)


def forward_kernel(
    coords_ref, bounds_ref, step_ref, depth_ref, w_in_ref, w_mid_ref, w_out_ref, bias_ref,
    seg_ref, enc_ref, h1_ref, h2_ref, s1_ref, s2_ref, raw_ref,
    w1_ref, w2_ref, b2_ref, wide_ref, scale_ref, pos_ref,
):
    slots, rays = step_ref.shape[1], step_ref.shape[2]
    freqs = w_in_ref.shape[1] // 6

    @pl.when(pl.program_id(0) == 0)
    def _():
        wide_ref[...] = jnp.zeros_like(wide_ref)
        w_in = w_in_ref[0].astype(jnp.float32) * 0.5
        for part in range(2):
            for l in range(freqs):
                to = part * 32 + (l % 2) * 16 + (l // 2) * 3
                at = part * 3 * freqs + l * 3
                wide_ref[to : to + 3, :] = w_in[at : at + 3, :]
        half_bias = bias_ref[0] * 0.5
        upper = half_bias[0:1].astype(jnp.bfloat16).astype(jnp.float32)
        wide_ref[47:48, :] = upper
        wide_ref[63:64, :] = half_bias[0:1] - upper
        w1_ref[...] = wide_ref[...].T.astype(jnp.bfloat16)
        w2_ref[...] = (w_mid_ref[0].astype(jnp.float32) * 0.5).T.astype(jnp.bfloat16)
        b2_ref[...] = jnp.broadcast_to(half_bias[1:2], (LANES, half_bias.shape[1])).T
        row = lax.broadcasted_iota(jnp.int32, scale_ref.shape, 0)
        scale = jnp.zeros(scale_ref.shape, jnp.float32)
        for l in range(0, freqs, 2):
            scale = jnp.where(row // 3 == l // 2, 2.0 ** (l - 1), scale)
        scale_ref[...] = scale

    for c in range(3):
        p = (coords_ref[c, 0].astype(jnp.float32) + 0.5) * (1.0 / GRID)
        angle = p * math.pi
        error = ((angle - p * PI_HI) - p * PI_MID) - p * PI_LO
        pos_ref[c] = p
        pos_ref[3 + c] = error * (1.0 / math.pi)

    coord = lax.broadcasted_iota(jnp.int32, (16, rays), 0) % 3
    scale = scale_ref[...]
    b2 = jnp.concatenate([b2_ref[...]] * (rays // LANES), axis=1)
    for s in range(slots):
        rows = [jnp.broadcast_to(pos_ref[i, s : s + 1, :], (16, rays)) for i in range(6)]
        p = jnp.where(coord == 0, rows[0], jnp.where(coord == 1, rows[1], rows[2]))
        e = jnp.where(coord == 0, rows[3], jnp.where(coord == 1, rows[4], rows[5]))
        turns = p * scale
        r = (turns - jnp.round(turns)) + e * scale
        q = r * r
        sine = SIN_COEFS[4]
        for coef in SIN_COEFS[3::-1]:
            sine = sine * q + coef
        sine = sine * r
        cosine = COS_COEFS[3]
        for coef in COS_COEFS[2::-1]:
            cosine = cosine * q + coef
        cosine = cosine * q + 1.0
        twice = sine + sine
        sin_even = twice * cosine
        cos_even = 1.0 - twice * sine
        twice = sin_even + sin_even
        sin_odd = twice * cos_even
        cos_odd = 1.0 - twice * sin_even
        enc = jnp.concatenate([sin_even, sin_odd, cos_even, cos_odd], axis=0).astype(jnp.bfloat16)
        enc_ref[0, s] = enc

        def silu(half):
            w = jnp.tanh(half) + 1.0
            hidden = half * w
            return hidden.astype(jnp.bfloat16), (hidden * (2.0 - w) + w).astype(jnp.bfloat16)

        h1, s1 = silu(dot(w1_ref[...], enc))
        h1_ref[0, s] = h1
        s1_ref[0, s] = s1
        h2, s2 = silu(dot(w2_ref[...], h1) + b2)
        h2_ref[0, s] = h2
        s2_ref[0, s] = s2
        raw = dot(w_out_ref[0], h2)
        for c in range(4):
            raw_ref[0, c, s : s + 1, :] = raw[c : c + 1]

    raw = [raw_ref[0, c] for c in range(4)]
    step = step_ref[0]
    live, colour, optical, before, blend = ray_terms(raw, step, bounds_ref[0], bounds_ref[1])
    sums = [row_sum(blend * colour[c]) for c in range(3)]
    sums.append(row_sum(blend * depth_ref[0]))
    sums.append(-row_sum(optical))
    for j in range(rays // LANES):
        for i in range(5):
            seg_ref[j, i : i + 1, :] = sums[i][:, j * LANES : (j + 1) * LANES]


def join_kernel(region_ref, seg_ref, rank_ref, target_ref, out_ref, *, loss_scale):
    regions = seg_ref.shape[0]
    rank = rank_ref[...].astype(jnp.float32).T
    seg = [seg_ref[:, i, :] for i in range(5)]
    passing = jnp.zeros_like(rank)
    for r in range(regions):
        passing = passing + jnp.where(rank[r : r + 1] < rank, seg[4][r : r + 1], 0.0)
    light = jnp.exp(passing)
    grads = []
    weighted = jnp.zeros_like(light)
    for i in range(4):
        gain = 2.0 * loss_scale * (DEPTH_WEIGHT if i == 3 else 1.0)
        grad = gain * (row_sum(light * seg[i]) - target_ref[i : i + 1])
        grads.append(grad)
        weighted = weighted + grad * seg[i]
    terms = light * weighted
    later = jnp.zeros_like(terms)
    for r in range(regions):
        later = later + jnp.where(rank[r : r + 1] > rank, terms[r : r + 1], 0.0)
    for i in range(4):
        out_ref[:, i, :] = light * grads[i]
    out_ref[:, 4, :] = later


def backward_kernel(
    grad_ref, bounds_ref, step_ref, depth_ref, w_mid_ref, w_out_ref,
    enc_ref, h1_ref, h2_ref, s1_ref, s2_ref, raw_ref,
    out_ref,
    wm_ref, wo_ref, mid_ref, in_ref, outer_ref, bias_ref, gr_ref,
):
    slots, rays = step_ref.shape[1], step_ref.shape[2]

    @pl.when(pl.program_id(0) == 0)
    def _():
        wm_ref[...] = (w_mid_ref[0].astype(jnp.float32) * 0.5).astype(jnp.bfloat16)
        w_out = w_out_ref[0].astype(jnp.float32) * 0.5
        w_out = jnp.concatenate([w_out, jnp.zeros_like(w_out)], axis=0)
        wo_ref[...] = w_out.T.astype(jnp.bfloat16)
        mid_ref[...] = jnp.zeros_like(mid_ref)
        in_ref[...] = jnp.zeros_like(in_ref)
        outer_ref[...] = jnp.zeros_like(outer_ref)
        bias_ref[...] = jnp.zeros_like(bias_ref)
        gr_ref[...] = jnp.zeros_like(gr_ref)

    raw = [raw_ref[0, c] for c in range(4)]
    step = step_ref[0]
    live, colour, optical, before, blend = ray_terms(raw, step, bounds_ref[0], bounds_ref[1])
    grad = [
        jnp.concatenate([grad_ref[j, i : i + 1, :] for j in range(rays // LANES)], axis=1)
        for i in range(5)
    ]
    usage = grad[3] * depth_ref[0]
    for c in range(3):
        usage = usage + grad[c] * colour[c]
    weighted = usage * blend
    later = row_sum(weighted) - (shift_down(weighted) + weighted)
    grad_optical = usage * jnp.exp(-(before + optical)) - later - grad[4]
    grad_raw = [grad_optical * step * live * sigmoid(raw[0])]
    for c in range(3):
        grad_raw.append(grad[c] * blend * colour[c] * (1.0 - colour[c]))
    for s in range(slots):
        for c in range(4):
            gr_ref[s, c : c + 1, :] = grad_raw[c][s : s + 1]

    for s in range(slots):
        gr = gr_ref[s].astype(jnp.bfloat16)
        grad_two = dot(wo_ref[...], gr) * s2_ref[0, s].astype(jnp.float32)
        partial = bias_ref[...]
        for j in range(rays // LANES):
            partial = partial + grad_two[:, j * LANES : (j + 1) * LANES]
        bias_ref[...] = partial
        d2 = grad_two.astype(jnp.bfloat16)
        grad_one = dot(wm_ref[...], d2) * s1_ref[0, s].astype(jnp.float32)
        d1 = grad_one.astype(jnp.bfloat16)
        mid_ref[...] += dot_nt(d2, h1_ref[0, s])
        in_ref[...] += dot_nt(enc_ref[0, s], d1)
        outer_ref[...] += dot_nt(gr, h2_ref[0, s])

    @pl.when(pl.program_id(0) == pl.num_programs(0) - 1)
    def _():
        hid = mid_ref.shape[0]
        bias = jnp.sum(bias_ref[...], axis=1, keepdims=True)
        rest = jnp.concatenate([in_ref[...], outer_ref[...]], axis=0)
        rest = jnp.concatenate([rest, jnp.zeros((LANES - rest.shape[0], hid), jnp.float32)], axis=0).T
        lane = lax.broadcasted_iota(jnp.int32, rest.shape, 1)
        rest = jnp.where(lane == LANES - 1, bias, rest)
        parts, width = out_ref.shape[0], out_ref.shape[1]
        for k in range(parts):
            out_ref[k, :, :hid] = mid_ref[k * width : (k + 1) * width, :]
            out_ref[k, :, hid:] = rest[k * width : (k + 1) * width, :]


def finish_kernel(parts_ref, in_ref, mid_ref, out_ref, bias_ref):
    total = parts_ref[0]
    for k in range(1, parts_ref.shape[0]):
        total = total + parts_ref[k]
    hid = mid_ref.shape[1]
    freqs = in_ref.shape[1] // 6
    mid_ref[0] = total[:, :hid].T
    rest = total[:, hid:].T
    for part in range(2):
        for l in range(freqs):
            to = part * 32 + (l % 2) * 16 + (l // 2) * 3
            at = part * 3 * freqs + l * 3
            in_ref[0, at : at + 3, :] = rest[to : to + 3, :]
    out_ref[0] = rest[ENC_ROWS : ENC_ROWS + 4, :]
    bias_ref[0, 0:1, :] = rest[47:48, :]
    bias_ref[0, 1:2, :] = rest[LANES - 1 : LANES, :]


def whole(shape):
    return pl.BlockSpec(shape, lambda *_: (0,) * len(shape))


def on_device(
    grid_coords, segment_bounds, depth_rank, step_length, sample_depth,
    target_pixels, weight_in, weight_mid, weight_out, bias_hidden,
):
    f32, bf16 = jnp.float32, jnp.bfloat16
    _, slots, ray_count = step_length.shape
    regions = depth_rank.shape[1]
    enc, hid = weight_in.shape[1:]
    ways = lax.axis_size("rays")
    loss_scale = 1.0 / math.sqrt(ray_count * ways)
    rays = 512
    tiles = ray_count // rays
    chunk = rays // LANES
    arbitrary = pltpu.CompilerParams(dimension_semantics=("arbitrary",))

    ray_specs = [
        pl.BlockSpec((2, 1, rays), lambda t: (0, 0, t)),
        pl.BlockSpec((1, slots, rays), lambda t: (0, 0, t)),
        pl.BlockSpec((1, slots, rays), lambda t: (0, 0, t)),
    ]
    seg_spec = pl.BlockSpec((chunk, 8, LANES), lambda t: (t, 0, 0))
    save_specs = [
        pl.BlockSpec((1, slots, n, rays), lambda t: (t, 0, 0, 0))
        for n in (ENC_ROWS, hid, hid, hid, hid)
    ] + [pl.BlockSpec((1, 4, slots, rays), lambda t: (t, 0, 0, 0))]
    save_shapes = [
        jax.ShapeDtypeStruct((tiles, slots, n, rays), bf16) for n in (ENC_ROWS, hid, hid, hid, hid)
    ] + [jax.ShapeDtypeStruct((tiles, 4, slots, rays), f32)]

    outs = pl.pallas_call(
        forward_kernel,
        grid=(tiles,),
        in_specs=[pl.BlockSpec((3, 1, slots, rays), lambda t: (0, 0, 0, t))]
        + ray_specs
        + [whole(weight_in.shape), whole(weight_mid.shape), whole(weight_out.shape), whole(bias_hidden.shape)],
        out_specs=[seg_spec] + save_specs,
        out_shape=[jax.ShapeDtypeStruct((ray_count // LANES, 8, LANES), f32)] + save_shapes,
        scratch_shapes=[
            pltpu.VMEM((hid, ENC_ROWS), bf16),
            pltpu.VMEM((hid, hid), bf16),
            pltpu.VMEM((hid, LANES), f32),
            pltpu.VMEM((ENC_ROWS, hid), f32),
            pltpu.VMEM((16, rays), f32),
            pltpu.VMEM((6, slots, rays), f32),
        ],
        compiler_params=arbitrary,
        name="forward",
    )(grid_coords, segment_bounds, step_length, sample_depth, weight_in, weight_mid, weight_out, bias_hidden)
    segment, saved = outs[0], outs[1:]

    segments = lax.all_to_all(segment, "region", 0, 0, tiled=True)
    own = ray_count // regions
    position = lax.axis_index("region").astype(jnp.int32).reshape(1)
    joined = pl.pallas_call(
        functools.partial(join_kernel, loss_scale=loss_scale),
        grid_spec=pltpu.PrefetchScalarGridSpec(
            num_scalar_prefetch=1,
            grid=(1,),
            in_specs=[
                pl.BlockSpec((regions, 8, own), lambda t, at: (0, 0, 0)),
                pl.BlockSpec((own, regions), lambda t, at: (at[0], 0)),
                pl.BlockSpec((4, own), lambda t, at: (0, at[0])),
            ],
            out_specs=pl.BlockSpec((regions, 8, own), lambda t, at: (0, 0, 0)),
        ),
        out_shape=jax.ShapeDtypeStruct((regions, 8, own), f32),
        compiler_params=arbitrary,
        name="join",
    )(position, segments, depth_rank, target_pixels)
    segment_grad = lax.all_to_all(joined, "region", 0, 0, tiled=True)

    width = hid // ways
    grads = pl.pallas_call(
        backward_kernel,
        grid=(tiles,),
        in_specs=[seg_spec] + ray_specs + [whole(weight_mid.shape), whole(weight_out.shape)] + save_specs,
        out_specs=whole((ways, width, hid + LANES)),
        out_shape=jax.ShapeDtypeStruct((ways, width, hid + LANES), f32),
        scratch_shapes=[
            pltpu.VMEM((hid, hid), bf16),
            pltpu.VMEM((hid, 8), bf16),
            pltpu.VMEM((hid, hid), f32),
            pltpu.VMEM((ENC_ROWS, hid), f32),
            pltpu.VMEM((8, hid), f32),
            pltpu.VMEM((hid, LANES), f32),
            pltpu.VMEM((slots, 8, rays), f32),
        ],
        compiler_params=arbitrary,
        name="backward",
    )(segment_grad, segment_bounds, step_length, sample_depth, weight_mid, weight_out, *saved)

    parts = lax.all_to_all(grads, "rays", 0, 0, tiled=True)
    return tuple(
        pl.pallas_call(
            finish_kernel,
            out_shape=[
                jax.ShapeDtypeStruct((1, n, width), f32) for n in (enc, hid, 4, 2)
            ],
            name="finish",
        )(parts)
    )


def solution(mesh):
    placed = (
        P(None, "region", None, "rays"),
        P(None, "region", "rays"),
        P("rays", None),
        P("region", None, "rays"),
        P("region", None, "rays"),
        P(None, "rays"),
        P("region", None, None),
        P("region", None, None),
        P("region", None, None),
        P("region", None, None),
    )
    return jax.shard_map(
        on_device,
        mesh=mesh,
        in_specs=placed,
        out_specs=(P("region", None, "rays"),) * 4,
        check_vma=False,
    )
```

time: 375 us -> 106 us (0.28)
  the two profiles are of different devices: /device:TPU:8 before, /device:TPU:1 now
where the time goes in v1:
time: 106 us; the launch traced here: 105 us
  Pallas kernels  49.7 us (47%)
  blocking collectives  29.6 us (28%)
  starting transfers between devices  12 us (11%)
  local copies, waits for them, and re-layouts  6.71 us (6%)
  waiting for transfers between devices  6.31 us (6%)
    pallas_call x1, Pallas kernels, on_device(): pl.pallas_call(forward_kernel, grid=(tiles,), in_specs=[pl.BlockSpec((3,...  24.4 us
    pallas_call x1, Pallas kernels, on_device(): pl.pallas_call(backward_kernel, grid=(tiles,), in_specs=[seg_spec] + ray_...  21.7 us
    all_to_all x1, blocking collectives, on_device(): parts = lax.all_to_all(grads, 'rays', 0, 0, tiled=True)  15.7 us
    all_to_all x1, blocking collectives, on_device(): segment_grad = lax.all_to_all(joined, 'region', 0, 0, tiled=True)  14 us
    all_to_all x1, starting transfers between devices, on_device(): segments = lax.all_to_all(segment, 'region', 0, 0, tiled=True)  12 us
    all_to_all x1, waiting for transfers between devices, on_device(): segments = lax.all_to_all(segment, 'region', 0, 0, tiled=True)  6.31 us
    unnamed x3, local copies, waits for them, and re-layouts  3.68 us
    pallas_call x2, local copies, waits for them, and re-layouts, on_device(): pl.pallas_call(finish_kernel, out_shape=[jax.ShapeDtypeStruct((1, n, widt...  3.03 us
  transfers between devices with their start and end apart: 1, of which 1 were waited for; matrix products, arithmetic and copies ran while one was open for 3% of the time, Pallas kernels for 0%

profile of v1, /device:TPU:1, one launch (start us, length us, event | category | flops | bytes accessed | tf_op | source)
XLA Modules:
  0.0 105.1 jit_solution(5713732463689844507)
XLA Ops:
  0.6 24.4 %forward.1 = (f32[32,8,128]{2,1,0:T(8,128)}, bf16[8,4,64,512]{3,2,1,0:T(8,128)(2,1)}, bf16[8,4,256,512]{3,2,1,0:T(8,128)(2,1)}, bf16[8,4,256,512]{3,2,1,0:T(8,12...) custom-call(s32[3,1,4,4096]{3,2,1,0:T(4,128)} %coords_ref.1, ...), custom_call_target="tpu_custom_call" | custom-call | tf_op jit(solution)/shard_map/forward/pallas_call | solution.py:312
  25.0 12.0 %all-to-all-start = ((f32[32,8,128]{2,1,0:T(8,128)}), f32[32,8,128]{2,1,0:T(8,128)S(1)}, u32[]{:S(2)}, u32[]{:S(2)}) async-start(f32[32,8,128]{2,1,0:T(8,128)} %get-tuple-element.11), calls=%async_computation | async-start | bytes 262144 | tf_op jit(solution)/shard_map/all_to_all | solution.py:333
  37.1 3.0 %copy.14.rank_ref = s32[4096,32]{1,0:T(8,128)} copy(s32[4096,32]{0,1:T(8,128)} %param.12) | data formatting | bytes 1048576 | tf_op args[2]
  40.1 6.3 %all-to-all-done.seg_ref = f32[32,8,128]{2,1,0:T(8,128)S(1)} async-done(((f32[32,8,128]{2,1,0:T(8,128)}), f32[32,8,128]{2,1,0:T(8,128)S(1)}, u32[]{:S(2)}, u32[]{:S(2)}) %all-to-all-start) | async-done | bytes 131104 | tf_op jit(solution)/shard_map/all_to_all | solution.py:333
  46.4 0.0 copy-start
  46.4 0.6 copy-done
  47.1 1.9 %join.1 = f32[32,8,128]{2,1,0:T(8,128)} custom-call(s32[1]{0:T(128)} %bitcast.region_ref, f32[32,8,128]{2,1,0:T(8,128)} %copy-done, s32[4096,32]{1,0:T(8,128)} %copy.14.rank_ref, f32[4,4096]{1,0:T(4,128)} %target_ref.1), custom_call_target="tpu_custom_call" | custom-call | tf_op jit(solution)/shard_map/join/pallas_call | solution.py:336
  48.9 14.0 %all_to_all.15.grad_ref = f32[32,8,128]{2,1,0:T(8,128)} all-to-all(f32[32,8,128]{2,1,0:T(8,128)} %join.1), channel_id=1, replica_groups=mesh['region'=32,'rays'=8] {'region'}, dimensions={0} | all-to-all | bytes 262144 | tf_op jit(solution)/shard_map/all_to_all | solution.py:352
  62.9 21.7 %backward.1 = f32[8,32,384]{2,1,0:T(8,128)} custom-call(f32[32,8,128]{2,1,0:T(8,128)} %all_to_all.15.grad_ref, s32[2,1,4096]{2,1,0:T(1,128)} %bounds_ref.3, f32[1,4,4096]{2,1,0:T(4,128)} %step_ref.3, f32[1,4,4096]{2,1,0:T(4,128)} %depth_ref.3, bf16[1,256,256]{2,1,0:T(8,128)(2,1)} %w_mid_ref.3, bf16[1,4,256]{2,1,0:T(4,128)(2,1)} %w_out_ref.3, ...), custom_call_target="tpu_custom_call" | custom-call | tf_op jit(solution)/shard_map/backward/pallas_call | solution.py:355
  84.6 15.7 %all_to_all.16.parts_ref = f32[8,32,384]{2,1,0:T(8,128)} all-to-all(f32[8,32,384]{2,1,0:T(8,128)} %backward.1), channel_id=1, replica_groups=mesh['region'=32,'rays'=8] {'rays'}, dimensions={0} | all-to-all | bytes 786432 | tf_op jit(solution)/shard_map/all_to_all | solution.py:374
  100.2 1.8 %finish.1 = (f32[1,60,32]{2,1,0:T(8,128)}, f32[1,256,32]{2,1,0:T(8,128)}, f32[1,4,32]{2,1,0:T(4,128)}, f32[1,2,32]{2,1,0:T(2,128)}) custom-call(f32[8,32,384]{2,1,0:T(8,128)} %all_to_all.16.parts_ref), custom_call_target="tpu_custom_call" | custom-call | tf_op jit(solution)/shard_map/finish/pallas_call | solution.py:376
  102.0 1.6 %copy.16 = f32[1,256,32]{1,2,0:T(8,128)} copy(f32[1,256,32]{2,1,0:T(8,128)} %get-tuple-element.19) | data formatting | bytes 65536 | tf_op jit(solution)/shard_map/finish/pallas_call | solution.py:376
  103.6 1.4 %copy.15 = f32[1,60,32]{1,2,0:T(8,128)} copy(f32[1,60,32]{2,1,0:T(8,128)} %get-tuple-element.18) | data formatting | bytes 15360 | tf_op jit(solution)/shard_map/finish/pallas_call | solution.py:376
Async XLA Ops:
  25.0 21.4 %all-to-all-start = ((f32[32,8,128]{2,1,0:T(8,128)}), f32[32,8,128]{2,1,0:T(8,128)S(1)}, u32[]{:S(2)}, u32[]{:S(2)}) async-start(f32[32,8,128]{2,1,0:T(8,128)} %get-tuple-element.11), calls=%async_computation | async-start | bytes 262144 | tf_op jit(solution)/shard_map/all_to_all | solution.py:333
  46.4 0.6 copy-start
